TPU v7x, 512 devices: a whole 4x4x16 slice. The times are simulated.
512 devices in a mesh: row: 16 (over y, x), col: 16 (over z), depth: 2 (over core).
Axes of the slice: x: 4, y: 4, z: 16, core: 2. Of those that a mesh axis runs over, the one named last changes fastest.
Arguments:
- features: bfloat16 [2, 16384, 1024], P('depth', ('row', 'col')), may hold values from -1.0546875 to 1.0546875
Outputs:
- drift: float32 [16384, 16384], P(('row', 'depth'), 'col')
All inputs are finite; a program needn't handle non-finite values.
Results may differ from a plain program's by a relative error of at most 0.0003.
Values may be sent and summed in bfloat16 or wider, within the bound.
No kernel may reach another device: no remote copies, remote signals or barrier semaphores. Data moves between devices by JAX's collectives and lax.ppermute only.
A program may use at most 64 MiB of HBM per device.

v0:
```python
import jax
import jax.numpy as jnp
from jax import lax
from jax.sharding import PartitionSpec as P


def broadcast(value, axis, source):
    kept = jnp.where(lax.axis_index(axis) == source, value, 0).astype(value.dtype)
    return lax.psum(kept, axis)


def transposed_product(left_rows, right_rows):
    return lax.dot_general(
        left_rows, right_rows, (((1,), (1,)), ((), ())), preferred_element_type=jnp.float32
    )


def body(features):
    rows_of = lax.axis_size("row")
    cols_of = lax.axis_size("col")
    own_shard = features[0]
    ex_dev = own_shard.shape[0]
    feat_width = own_shard.shape[1]
    per_dest = ex_dev // cols_of
    grouped = own_shard.reshape(cols_of, per_dest, 1, feat_width)
    row_piece = lax.all_to_all(grouped, "col", split_axis=0, concat_axis=2, tiled=True)
    row_block = lax.all_gather(row_piece.reshape(ex_dev, feat_width), "col", axis=0, tiled=True)
    col_ratio = cols_of // rows_of
    col_index = lax.axis_index("col")
    col_block = broadcast(row_block, "row", col_index // col_ratio)
    depth_index = lax.axis_index("depth")
    signum = 2.0 * depth_index.astype(jnp.float32) - 1.0
    return lax.psum_scatter(
        signum * transposed_product(row_block, col_block), "depth", scatter_dimension=0, tiled=True
    )


def solution(mesh):
    placed = (P("depth", ("row", "col"), None),)
    return jax.shard_map(
        body, mesh=mesh, in_specs=placed, out_specs=P(("row", "depth"), "col"), check_vma=False
    )
```

profile of v0, /device:TPU:1, one launch (start us, length us, event | category | flops | bytes accessed | tf_op | source)
XLA Modules:
  0.0 265.4 jit_solution(9115069896049042623)
XLA Ops:
  6.5 0.0 all-gather.2.cloned.1.call-start
  6.5 1.0 reshape_squeeze.3
  7.5 27.5 %all_to_all.15 = bf16[16,4,1,1024]{3,1,2,0:T(4,128)(2,1)S(1)} all-to-all(bf16[16,4,1,1024]{3,1,2,0:T(4,128)(2,1)S(1)} %bitcast.11), channel_id=1, replica_groups=mesh['row'=16,'col'=16,'depth'=2] {'col'}, dimensions={0} | all-to-all | bytes 262144 | tf_op jit(solution)/shard_map/all_to_all | solution.py:26
  35.0 0.7 copy.7
  35.7 0.0 all-gather.2.cloned.1.call-update
  35.8 0.0 all-reduce.2.cloned.1.call-start
  35.8 60.2 %all-gather.2.cloned.1.call-done = bf16[1024,1024]{1,0:T(8,128)(2,1)} async-done(((bf16[64,1024]{1,0:T(8,128)(2,1)}), bf16[1024,1024]{1,0:T(8,128)(2,1)}) %all-gather.2.cloned.1.call-update) | async-done | bytes 2097168 | tf_op jit(solution)/shard_map/all_gather | solution.py:27
  96.1 3.0 %broadcast_select_fusion = bf16[1024,1024]{1,0:T(8,128)(2,1)} fusion(bf16[1024,1024]{1,0:T(8,128)(2,1)} %all-gather.2.cloned.1.call-done, pred[]{:T(512)S(6)} %eq.3), kind=kLoop, calls=%fused_computation.1 | loop fusion | flops 1048576 | bytes 4194305 | tf_op jit(solution)/shard_map/jit(_where)/select_n | solution.py:8
  99.1 0.0 copy-start
  99.1 0.0 all-reduce.2.cloned.1.call-update
  99.1 0.0 reduce-scatter.2.cloned.1.call-start
  99.2 126.3 %all-reduce.2.cloned.1.call-done = bf16[1024,1024]{1,0:T(8,128)(2,1)} async-done(((bf16[1024,1024]{1,0:T(8,128)(2,1)}), bf16[1024,1024]{1,0:T(8,128)(2,1)}) %all-reduce.2.cloned.1.call-update) | async-done | bytes 2097168 | tf_op jit(solution)/shard_map/psum | solution.py:9
  225.5 0.0 copy-done
  225.5 5.9 %multiply_bitcast_fusion = f32[1024,1024]{0,1:T(8,128)} fusion(bf16[1024,1024]{1,0:T(8,128)(2,1)} %all-reduce.2.cloned.1.call-done, bf16[1024,1024]{1,0:T(8,128)(2,1)S(1)} %copy-done, f32[]{:T(128)S(6)} %sub.5), kind=kOutput, calls=%fused_computation | convolution fusion | flops 2148532224 | bytes 8388612 | tf_op jit(solution)/shard_map/dot_general | solution.py:13
  231.4 0.0 reduce-scatter.2.cloned.1.call-update
  231.4 24.6 %reduce-scatter.2.cloned.1.call-done = f32[512,1024]{0,1:T(8,128)} async-done(((f32[1024,1024]{0,1:T(8,128)}), f32[512,1024]{0,1:T(8,128)}) %reduce-scatter.2.cloned.1.call-update) | async-done | bytes 2097168 | tf_op jit(solution)/shard_map/reduce_scatter | solution.py:33
  256.0 2.9 %copy.8 = f32[512,1024]{1,0:T(8,128)} copy(f32[512,1024]{0,1:T(8,128)} %reduce-scatter.2.cloned.1.call-done) | data formatting | bytes 4194304 | tf_op jit(solution)/shard_map/reduce_scatter | solution.py:33
Async XLA Ops:
  6.5 89.5 %all-gather.2.cloned.1.call-start = ((), (), s32[]{:S(2)}) async-start(), calls=%async_computation.2 | async-start | bytes 2228224 | tf_op jit(solution)/shard_map/all_gather | solution.py:27
  35.8 189.7 %all-reduce.2.cloned.1.call-start = ((), (), s32[]{:S(2)}) async-start(), calls=%async_computation.3 | async-start | bytes 4194304 | tf_op jit(solution)/shard_map/psum | solution.py:9
  99.1 126.4 %copy-start = (bf16[1024,1024]{1,0:T(8,128)(2,1)S(1)}, bf16[1024,1024]{1,0:T(8,128)(2,1)}, u32[]{:S(2)}) copy-start(bf16[1024,1024]{1,0:T(8,128)(2,1)} %all-gather.2.cloned.1.call-done) | copy-start | bytes 6291460
  99.1 156.8 %reduce-scatter.2.cloned.1.call-start = ((), (), s32[]{:S(2)}) async-start(), calls=%async_computation.4 | async-start | bytes 6291456 | tf_op jit(solution)/shard_map/reduce_scatter | solution.py:33
Sparse Core Ops, SparseCore 0:
  35.9 60.1 all-gather.1
  99.4 126.0 all-reduce.1
  231.5 24.4 reduce-scatter.1
where the time goes:
time: 266 us; the launch traced here: 265 us
  waiting for transfers between devices  211 us (79%)
  blocking collectives  27.5 us (10%)
  between operations  13.1 us (5%)
  matrix products  5.9 us (2%)
  local copies, waits for them, and re-layouts  4.54 us (2%)
  other arithmetic  3.05 us (1%)
    psum x1, waiting for transfers between devices, broadcast(): return lax.psum(kept, axis)  126 us
    all_gather x1, waiting for transfers between devices, body(): lax.all_gather(row_piece.reshape(ex_dev, feat_width), 'col', axis=0, tile...  60.2 us
    all_to_all x1, blocking collectives, body(): lax.all_to_all(grouped, 'col', split_axis=0, concat_axis=2, tiled=True)  27.5 us
    reduce_scatter x1, waiting for transfers between devices, body(): lax.psum_scatter(signum * transposed_product(row_block, col_block), 'dept...  24.6 us
    dot_general x1, matrix products, transposed_product(): lax.dot_general(left_rows, right_rows, (((1,), (1,)), ((), ())), preferre...  5.9 us
  transfers between devices with their start and end apart: 3, of which 3 were waited for; matrix products, arithmetic and copies ran while one was open for 0% of the time, Pallas kernels for 0%

commit v1 on v0

--- a/solution.py
+++ b/solution.py
@@ -6,7 +6,11 @@
 
 def broadcast(value, axis, source):
     kept = jnp.where(lax.axis_index(axis) == source, value, 0).astype(value.dtype)
-    return lax.psum(kept, axis)
+
+    def lift_joints_all(axis_key, incoming_x):
+        return lax.all_gather(incoming_x, axis_key).sum(axis=0)
+
+    return lift_joints_all(axis, kept)
 
 
 def transposed_product(left_rows, right_rows):

time: 266 us -> 369 us (1.39)
  waiting for transfers between devices: 211 us -> 303 us
  other arithmetic: 3.05 us -> 14.8 us
    all_gather x0 -> x1, waiting for transfers between devices: none -> 218 us  [lift_joints_all(): return lax.all_gather(incoming_x, axis_key).sum(axis=0)]
    psum x1 -> x0, waiting for transfers between devices: 126 us -> none  [broadcast(): return lax.psum(kept, axis)]
    reduce_sum x0 -> x1, other arithmetic: none -> 11.7 us  [lift_joints_all(): return lax.all_gather(incoming_x, axis_key).sum(axis=0)]
where the time goes in v1:
time: 369 us
  waiting for transfers between devices  303 us (82%)
  blocking collectives  27.5 us (7%)
  other arithmetic  14.8 us (4%)
  between operations  13.1 us (4%)
  matrix products  5.9 us (2%)
  local copies, waits for them, and re-layouts  4.54 us (1%)
    all_gather x1, waiting for transfers between devices, lift_joints_all(): return lax.all_gather(incoming_x, axis_key).sum(axis=0)  218 us
    all_gather x1, waiting for transfers between devices, body(): lax.all_gather(row_piece.reshape(ex_dev, feat_width), 'col', axis=0, tile...  60.2 us
    all_to_all x1, blocking collectives, body(): lax.all_to_all(grouped, 'col', split_axis=0, concat_axis=2, tiled=True)  27.5 us
    reduce_scatter x1, waiting for transfers between devices, body(): lax.psum_scatter(signum * transposed_product(row_block, col_block), 'dept...  23.8 us
    reduce_sum x1, other arithmetic, lift_joints_all(): return lax.all_gather(incoming_x, axis_key).sum(axis=0)  11.7 us
  transfers between devices with their start and end apart: 3, of which 3 were waited for; matrix products, arithmetic and copies ran while one was open for 0% of the time, Pallas kernels for 0%

profile of v1, /device:TPU:1, one launch (start us, length us, event | category | flops | bytes accessed | tf_op | source)
XLA Modules:
  0.0 368.5 jit_solution(10441704763632106798)
XLA Ops:
  6.5 0.0 all-gather.4.cloned.1.call-start
  6.5 1.0 reshape_squeeze.3
  7.5 27.5 %all_to_all.15 = bf16[16,4,1,1024]{3,1,2,0:T(4,128)(2,1)S(1)} all-to-all(bf16[16,4,1,1024]{3,1,2,0:T(4,128)(2,1)S(1)} %bitcast.13), channel_id=1, replica_groups=mesh['row'=16,'col'=16,'depth'=2] {'col'}, dimensions={0} | all-to-all | bytes 262144 | tf_op jit(solution)/shard_map/all_to_all | solution.py:30
  35.0 0.7 copy.7
  35.7 0.0 all-gather.4.cloned.1.call-update
  35.8 0.0 all-gather.6.cloned.1.call-start
  35.8 60.2 %all-gather.4.cloned.1.call-done = bf16[1024,1024]{1,0:T(8,128)(2,1)} async-done(((bf16[64,1024]{1,0:T(8,128)(2,1)}), bf16[1024,1024]{1,0:T(8,128)(2,1)}) %all-gather.4.cloned.1.call-update) | async-done | bytes 2097168 | tf_op jit(solution)/shard_map/all_gather | solution.py:31
  96.1 3.0 broadcast_select_fusion
  99.1 0.0 all-gather.6.cloned.1.call-update
  99.1 0.0 reduce-scatter.2.cloned.1.call-start
  99.2 218.4 %all-gather.6.cloned.1.call-done = bf16[16384,1024]{1,0:T(8,128)(2,1)} async-done(((bf16[1024,1024]{1,0:T(8,128)(2,1)}), bf16[16384,1024]{1,0:T(8,128)(2,1)}) %all-gather.6.cloned.1.call-update) | async-done | bytes 33554448 | tf_op jit(solution)/shard_map/all_gather | solution.py:11
  317.6 11.7 %reduce_sum.12 = bf16[1024,1024]{1,0:T(8,128)(2,1)S(1)} reduce(bf16[16,1024,1024]{2,1,0:T(8,128)(2,1)} %bitcast.11, bf16[]{:T(256)} %constant.32.clone.1), dimensions={0}, to_apply=%region_0.1 | reduce | flops 15728640 | bytes 35651584 | tf_op jit(solution)/shard_map/reduce_sum | solution.py:11
  329.4 5.9 %multiply_bitcast_fusion = f32[1024,1024]{0,1:T(8,128)} fusion(bf16[1024,1024]{1,0:T(8,128)(2,1)S(1)} %reduce_sum.12, bf16[1024,1024]{1,0:T(8,128)(2,1)} %all-gather.4.cloned.1.call-done, f32[]{:T(128)S(6)} %sub.5), kind=kOutput, calls=%fused_computation | convolution fusion | flops 2148532224 | bytes 8388612 | tf_op jit(solution)/shard_map/dot_general | solution.py:17
  335.3 0.0 reduce-scatter.2.cloned.1.call-update
  335.3 23.8 %reduce-scatter.2.cloned.1.call-done = f32[512,1024]{0,1:T(8,128)} async-done(((f32[1024,1024]{0,1:T(8,128)}), f32[512,1024]{0,1:T(8,128)}) %reduce-scatter.2.cloned.1.call-update) | async-done | bytes 2097168 | tf_op jit(solution)/shard_map/reduce_scatter | solution.py:37
  359.1 2.9 copy.8
Async XLA Ops:
  6.5 89.5 %all-gather.4.cloned.1.call-start = ((), (), s32[]{:S(2)}) async-start(), calls=%async_computation.2 | async-start | bytes 2228224 | tf_op jit(solution)/shard_map/all_gather | solution.py:31
  35.8 281.8 %all-gather.6.cloned.1.call-start = ((), (), s32[]{:S(2)}) async-start(), calls=%async_computation.4 | async-start | bytes 35651584 | tf_op jit(solution)/shard_map/all_gather | solution.py:11
  99.1 260.0 %reduce-scatter.2.cloned.1.call-start = ((), (), s32[]{:S(2)}) async-start(), calls=%async_computation.3 | async-start | bytes 6291456 | tf_op jit(solution)/shard_map/reduce_scatter | solution.py:37
Sparse Core Ops, SparseCore 0:
  35.9 60.1 all-gather.3
  99.3 218.3 all-gather.5
  335.4 23.6 reduce-scatter.1

commit v2 on v0

--- a/solution.py
+++ b/solution.py
@@ -2,6 +2,18 @@
 import jax.numpy as jnp
 from jax import lax
 from jax.sharding import PartitionSpec as P
+
+
+def cover_levels_all_now(obj, shard_axis):
+    return jnp.concatenate(
+        lax.all_to_all(
+            jnp.stack(lax.psum(1, shard_axis) * [obj], axis=0),
+            shard_axis,
+            split_axis=0,
+            concat_axis=0,
+        ),
+        axis=0,
+    )
 
 
 def broadcast(value, axis, source):
@@ -24,7 +36,7 @@
     per_dest = ex_dev // cols_of
     grouped = own_shard.reshape(cols_of, per_dest, 1, feat_width)
     row_piece = lax.all_to_all(grouped, "col", split_axis=0, concat_axis=2, tiled=True)
-    row_block = lax.all_gather(row_piece.reshape(ex_dev, feat_width), "col", axis=0, tiled=True)
+    row_block = cover_levels_all_now(row_piece.reshape(ex_dev, feat_width), "col")
     col_ratio = cols_of // rows_of
     col_index = lax.axis_index("col")
     col_block = broadcast(row_block, "row", col_index // col_ratio)

time: 266 us -> 297 us (1.12)
  waiting for transfers between devices: 211 us -> 237 us
  starting transfers between devices: 0.09 us -> 6.01 us
    all_to_all x0 -> x1, waiting for transfers between devices: none -> 91.8 us  [cover_levels_all_now(): lax.all_to_all(jnp.stack(lax.psum(1, shard_axis) * [obj], axis=0), shard_...]
    all_gather x1 -> x0, waiting for transfers between devices: 60.2 us -> none  [body(): lax.all_gather(row_piece.reshape(ex_dev, feat_width), 'col', axis=0, tile...]
    all_to_all x0 -> x1, starting transfers between devices: none -> 5.93 us  [cover_levels_all_now(): lax.all_to_all(jnp.stack(lax.psum(1, shard_axis) * [obj], axis=0), shard_...]
    psum x1, waiting for transfers between devices: 126 us -> 121 us  [broadcast(): return lax.psum(kept, axis)]
where the time goes in v2:
time: 297 us
  waiting for transfers between devices  237 us (80%)
  blocking collectives  27.5 us (9%)
  between operations  13.4 us (5%)
  starting transfers between devices  6.01 us (2%)
  matrix products  5.9 us (2%)
  local copies, waits for them, and re-layouts  5.47 us (2%)
    psum x1, waiting for transfers between devices, broadcast(): return lax.psum(kept, axis)  121 us
    all_to_all x1, waiting for transfers between devices, cover_levels_all_now(): lax.all_to_all(jnp.stack(lax.psum(1, shard_axis) * [obj], axis=0), shard_...  91.8 us
    all_to_all x1, blocking collectives, body(): lax.all_to_all(grouped, 'col', split_axis=0, concat_axis=2, tiled=True)  27.5 us
    reduce_scatter x1, waiting for transfers between devices, body(): lax.psum_scatter(signum * transposed_product(row_block, col_block), 'dept...  24.6 us
  transfers between devices with their start and end apart: 3, of which 3 were waited for; matrix products, arithmetic and copies ran while one was open for 0% of the time, Pallas kernels for 0%

profile of v2, /device:TPU:1, one launch (start us, length us, event | category | flops | bytes accessed | tf_op | source)
XLA Modules:
  0.0 296.9 jit_solution(8573551591369787447)
XLA Ops:
  6.5 1.0 reshape_squeeze.3
  7.5 27.5 %all_to_all.20 = bf16[16,4,1,1024]{3,1,2,0:T(4,128)(2,1)S(1)} all-to-all(bf16[16,4,1,1024]{3,1,2,0:T(4,128)(2,1)S(1)} %bitcast.14), channel_id=1, replica_groups=mesh['row'=16,'col'=16,'depth'=2] {'col'}, dimensions={0} | all-to-all | bytes 262144 | tf_op jit(solution)/shard_map/all_to_all | solution.py:38
  35.1 1.6 stack.3
  36.7 5.9 %all-to-all-start.1 = ((bf16[16,64,1024]{2,1,0:T(8,128)(2,1)}), bf16[16,64,1024]{2,1,0:T(8,128)(2,1)S(1)}, u32[]{:S(2)}, u32[]{:S(2)}) async-start(bf16[16,64,1024]{2,1,0:T(8,128)(2,1)} %stack.3), calls=%async_computation.1 | async-start | bytes 4194304 | tf_op jit(solution)/shard_map/all_to_all | solution.py:9
  42.6 0.0 all-reduce.2.cloned.1.call-start
  42.7 91.8 %all-to-all-done.1 = bf16[16,64,1024]{2,1,0:T(8,128)(2,1)S(1)} async-done(((bf16[16,64,1024]{2,1,0:T(8,128)(2,1)}), bf16[16,64,1024]{2,1,0:T(8,128)(2,1)S(1)}, u32[]{:S(2)}, u32[]{:S(2)}) %all-to-all-start.1) | async-done | bytes 2097184 | tf_op jit(solution)/shard_map/all_to_all | solution.py:9
  134.4 1.6 broadcast_select_fusion
  136.0 0.0 all-reduce.2.cloned.1.call-update
  136.1 0.0 reduce-scatter.2.cloned.1.call-start
  136.1 120.5 %all-reduce.2.cloned.1.call-done = bf16[1024,1024]{1,0:T(8,128)(2,1)} async-done(((bf16[1024,1024]{1,0:T(8,128)(2,1)}), bf16[1024,1024]{1,0:T(8,128)(2,1)}) %all-reduce.2.cloned.1.call-update) | async-done | bytes 2097168 | tf_op jit(solution)/shard_map/psum | solution.py:21
  256.7 5.9 %multiply_bitcast_fusion = f32[1024,1024]{0,1:T(8,128)} fusion(bf16[1024,1024]{1,0:T(8,128)(2,1)} %all-reduce.2.cloned.1.call-done, bf16[1024,1024]{1,0:T(8,128)(2,1)S(1)} %bitcast.12, f32[]{:T(128)S(6)} %sub.5), kind=kOutput, calls=%fused_computation | convolution fusion | flops 2148532224 | bytes 8388612 | tf_op jit(solution)/shard_map/dot_general | solution.py:25
  262.6 0.0 reduce-scatter.2.cloned.1.call-update
  262.6 24.6 %reduce-scatter.2.cloned.1.call-done = f32[512,1024]{0,1:T(8,128)} async-done(((f32[1024,1024]{0,1:T(8,128)}), f32[512,1024]{0,1:T(8,128)}) %reduce-scatter.2.cloned.1.call-update) | async-done | bytes 2097168 | tf_op jit(solution)/shard_map/reduce_scatter | solution.py:45
  287.2 2.9 copy.8
  (1 shorter events, 0.0 us)
Async XLA Ops:
  36.7 97.8 %all-to-all-start.1 = ((bf16[16,64,1024]{2,1,0:T(8,128)(2,1)}), bf16[16,64,1024]{2,1,0:T(8,128)(2,1)S(1)}, u32[]{:S(2)}, u32[]{:S(2)}) async-start(bf16[16,64,1024]{2,1,0:T(8,128)(2,1)} %stack.3), calls=%async_computation.1 | async-start | bytes 4194304 | tf_op jit(solution)/shard_map/all_to_all | solution.py:9
  42.6 214.0 %all-reduce.2.cloned.1.call-start = ((), (), s32[]{:S(2)}) async-start(), calls=%async_computation.3 | async-start | bytes 4194304 | tf_op jit(solution)/shard_map/psum | solution.py:21
  136.1 151.1 %reduce-scatter.2.cloned.1.call-start = ((), (), s32[]{:S(2)}) async-start(), calls=%async_computation.4 | async-start | bytes 6291456 | tf_op jit(solution)/shard_map/reduce_scatter | solution.py:45
Sparse Core Ops, SparseCore 0:
  136.2 120.4 all-reduce.1
  262.7 24.4 reduce-scatter.1
